TPU v7x, 32 devices: a whole 2x2x4 slice. The times are simulated.
32 devices in a mesh: gx: 4 (over y, x), gy: 8 (over z, core).
Axes of the slice: x: 2, y: 2, z: 4, core: 2. Of those that a mesh axis runs over, the one named last changes fastest.
Arguments:
- adjoint_start: float32 [4, 64, 128, 256], P(None, 'gx', 'gy'), may hold values from -6 to 6
- adjoint_source: float32 [4, 64, 128, 256], P(None, 'gx', 'gy'), may hold values from -6 to 6
- background_log_viscosity: float32 [64, 128, 256], P('gx', 'gy'), may hold values from -1 to 1
- background_density: float32 [64, 128, 256], P('gx', 'gy'), may hold values from 0.5 to 1.5
- marker_weights: float32 [4, 8, 32, 256], P('gx', 'gy'), may hold values from 0.1 to 2
- block_phase: int32 [4, 8, 32], P('gx', 'gy'), may hold values from 0 to 7
- block_owner: int32 [4, 8, 32], P('gx', 'gy'), may hold values from 0 to 3, as said below
- block_column: int32 [4, 8, 32], P('gx', 'gy'), may hold values from 0 to 255
- active_blocks: int32 [4, 8], P('gx', 'gy'), may hold values from 16 to 32
- phase_log_viscosity: float32 [8], replicated, may hold values from -1.5 to 1.5
- phase_density: float32 [8], replicated, may hold values from 0.5 to 2
Outputs:
- adjoint_end: float32 [4, 64, 128, 256], P(None, 'gx', 'gy')
- density_sensitivity: float32 [64, 128, 256], P('gx', 'gy')
Inputs may be any that keep to these rules, and one draw needn't show every extreme that they name: `block_owner`: among the blocks of one device at most 12 name the same owner. The first 12 blocks of every device are live and name one owner, the same for all devices of one gy index.
All inputs are finite; a program needn't handle non-finite values.
Results may differ from a plain program's by a relative error of at most 0.00009.
Values sent between devices are 32-bit elements; how exact they have to be, the bound alone decides.
A program may use at most 64 MiB of HBM per device.

v0:
```python
import jax
import jax.numpy as jnp
from jax import lax
from jax.sharding import PartitionSpec as P

RELAX_VELOCITY = 0.6
RELAX_PRESSURE = 0.5


def with_halo(cells, sides, width):
    for axis, dim in sides:
        count = lax.axis_size(axis)
        ends = count - 1
        head = lax.slice_in_dim(cells, 0, width, axis=dim)
        tail = lax.slice_in_dim(cells, cells.shape[dim] - width, cells.shape[dim], axis=dim)
        cells = jnp.concatenate(
            [
                lax.ppermute(tail, axis, [(i, (i + 1) % count) for i in range(ends)]),
                cells,
                lax.ppermute(head, axis, [((i + 1) % count, i) for i in range(ends)]),
            ],
            axis=dim,
        )
    return cells


def lookup(identity, table):
    matches = identity[..., None] == jnp.arange(table.shape[0], dtype=identity.dtype)
    return jnp.sum(jnp.where(matches, table, 0.0), axis=-1)


def neighbour(padded, axis_dim, step):
    extent = [padded.shape[0] - 2, padded.shape[1] - 2, padded.shape[2] - 2]
    offset = [1, 1, 1]
    offset[axis_dim] = offset[axis_dim] + step
    return padded[
        offset[0] : offset[0] + extent[0],
        offset[1] : offset[1] + extent[1],
        offset[2] : offset[2] + extent[2],
    ]


def smooth_once(field_pad, visc_pad, source):
    centre_visc = neighbour(visc_pad, 0, 0)
    upper_coef = [0.5 * (centre_visc + neighbour(visc_pad, axis_dim, 1)) for axis_dim in range(3)]
    lower_coef = [0.5 * (centre_visc + neighbour(visc_pad, axis_dim, -1)) for axis_dim in range(3)]
    diagonal = (
        upper_coef[0]
        + lower_coef[0]
        + upper_coef[1]
        + lower_coef[1]
        + upper_coef[2]
        + lower_coef[2]
    )
    pressure = field_pad[3]
    centre_press = neighbour(pressure, 0, 0)
    results = []
    divergence = jnp.zeros_like(centre_visc)
    for component in range(3):
        velocity = field_pad[component]
        centre = neighbour(velocity, 0, 0)
        viscous = jnp.zeros_like(centre)
        for axis_dim in range(3):
            viscous = viscous + upper_coef[axis_dim] * (centre - neighbour(velocity, axis_dim, 1))
            viscous = viscous + lower_coef[axis_dim] * (centre - neighbour(velocity, axis_dim, -1))
        pressure_push = neighbour(pressure, component, 1) - centre_press
        residual = source[component] - viscous - pressure_push
        results.append(centre + RELAX_VELOCITY * residual / diagonal)
        divergence = divergence + (centre - neighbour(velocity, component, -1))
    residual_press = source[3] + divergence
    results.append(centre_press - RELAX_PRESSURE * centre_visc * residual_press)
    return jnp.stack(results)


def depth_pad(stacked):
    return jnp.pad(stacked, ((0, 0), (0, 0), (0, 0), (1, 1)))


def plane_pad(single):
    return jnp.pad(single, ((0, 0), (0, 0), (1, 1)))


def on_device(
    adjoint_start,
    adjoint_source,
    background_log_viscosity,
    background_density,
    marker_weights,
    block_phase,
    block_owner,
    block_column,
    active_blocks,
    phase_log_viscosity,
    phase_density,
):
    owners = lax.axis_size("gx")
    blocks = marker_weights.shape[2]
    depth = marker_weights.shape[3]
    cells_x = background_density.shape[0]
    cells_y = background_density.shape[1]
    capacity = max(2, 3 * blocks // (2 * owners))
    weights = marker_weights[0, 0]
    phases = block_phase[0, 0]
    targets = block_owner[0, 0]
    columns = block_column[0, 0]
    active = jnp.arange(blocks, dtype=jnp.int32) < active_blocks[0, 0]
    matches = (targets[:, None] == jnp.arange(owners, dtype=jnp.int32)[None, :]) & active[:, None]
    match_int = matches.astype(jnp.int32)
    before = jnp.cumsum(match_int, axis=0) - match_int
    position = jnp.sum(jnp.where(matches, before, 0), axis=1)
    slot_index = targets * capacity + position
    selector = (
        (slot_index[None, :] == jnp.arange(owners * capacity, dtype=jnp.int32)[:, None])
        & active[None, :]
    ).astype(jnp.float32)
    highest = lax.Precision.HIGHEST
    payload = jnp.concatenate(
        [
            weights,
            weights * lookup(phases, phase_log_viscosity)[:, None],
            weights * lookup(phases, phase_density)[:, None],
        ],
        axis=1,
    )
    sent_rows = jnp.dot(selector, payload, precision=highest, preferred_element_type=jnp.float32)
    sent_meta = jnp.dot(
        selector,
        (columns + 1).astype(jnp.float32)[:, None],
        precision=highest,
        preferred_element_type=jnp.float32,
    )
    got_rows, got_meta = (
        lax.all_to_all(
            sent_rows.reshape(owners, capacity, 3 * depth),
            "gx",
            split_axis=0,
            concat_axis=0,
            tiled=True,
        ),
        lax.all_to_all(
            sent_meta.reshape(owners, capacity, 1), "gx", split_axis=0, concat_axis=0, tiled=True
        ),
    )
    received = got_rows.reshape(owners * capacity, 3 * depth)
    slot_column = got_meta.reshape(owners * capacity) - 1.0
    placing = (
        slot_column[None, :] == jnp.arange(cells_x * cells_y, dtype=jnp.float32)[:, None]
    ).astype(jnp.float32)
    summed = jnp.dot(
        placing, received, precision=highest, preferred_element_type=jnp.float32
    ).reshape(cells_x, cells_y, 3, depth)
    weight_sum = 1.0 + summed[:, :, 0]
    viscosity = jnp.exp((background_log_viscosity + summed[:, :, 1]) / weight_sum)
    density = (background_density + summed[:, :, 2]) / weight_sum
    rimmed = with_halo(
        jnp.concatenate([adjoint_start, viscosity[None]], axis=0), (("gx", 1), ("gy", 2)), 1
    )
    visc_pad = plane_pad(rimmed[4])
    first = smooth_once(depth_pad(rimmed[:4]), visc_pad, adjoint_source)
    second_rimmed = with_halo(first, (("gx", 1), ("gy", 2)), 1)
    final = smooth_once(depth_pad(second_rimmed), visc_pad, adjoint_source)
    return (final, density * final[2])


def solution(mesh):
    in_specs = (
        P(None, "gx", "gy", None),
        P(None, "gx", "gy", None),
        P("gx", "gy", None),
        P("gx", "gy", None),
        P("gx", "gy", None, None),
        P("gx", "gy", None),
        P("gx", "gy", None),
        P("gx", "gy", None),
        P("gx", "gy"),
        P(),
        P(),
    )
    out_specs = (P(None, "gx", "gy", None), P("gx", "gy", None))
    return jax.shard_map(
        on_device, mesh=mesh, in_specs=in_specs, out_specs=out_specs, check_vma=False
    )
```

profile of v0, /device:TPU:1, one launch (start us, length us, event | category | flops | bytes accessed | tf_op | source)
XLA Modules:
  0.0 71.2 jit_solution(3946144903543424492)
XLA Ops:
  0.6 0.0 copy-start.2
  0.6 0.0 copy-start
  1.4 0.7 %fusion.143 = s32[32,4]{1,0:T(8,128)S(1)} fusion(s32[32]{0:T(128)} %bitcast.131, pred[32]{0:T(512)(128)(4,1)S(1)} %iota_compare_fusion.3), kind=kLoop, calls=%fused_computation.232 | loop fusion | flops 384 | bytes 672 | tf_op jit(solution)/shard_map/convert_element_type | solution.py:108
  2.1 0.1 reduce_window_sum.11
  2.2 0.8 %select_reduce_fusion = s32[32]{0:T(128)S(1)} fusion(s32[32,4]{1,0:T(8,128)S(1)} %reduce_window_sum.11, s32[32]{0:T(128)} %bitcast.132, pred[32]{0:T(512)(128)(4,1)S(1)} %iota_compare_fusion.3), kind=kLoop, calls=%fused_computation.229 | loop fusion | flops 736 | bytes 800 | tf_op jit(solution)/shard_map/reduce_sum | solution.py:110
  3.0 0.7 multiply_add_fusion.2
  3.7 1.5 %convolution_bitcast_fusion = f32[4,12,1]{1,2,0:T(1,128)} fusion(s32[4,12]{1,0:T(4,128)S(1)} %multiply_add_fusion.1, s32[32]{0:T(128)S(1)} %multiply_add_fusion.2, pred[32]{0:T(512)(128)(4,1)S(1)} %iota_compare_fusion.3, s32[1,1,32]{2,1,0:T(1,128)} %param.18), kind=kOutput, calls=%fused_computation.10 | convolution fusion | flops 21568 | bytes 672 | tf_op jit(solution)/shard_map/dot_general | solution.py:126
  5.3 4.3 %all-to-all-start = ((f32[4,12,1]{1,2,0:T(1,128)}), f32[4,12,1]{1,2,0:T(1,128)S(1)}, u32[]{:S(2)}, u32[]{:S(2)}) async-start(f32[4,12,1]{1,2,0:T(1,128)} %convolution_bitcast_fusion), calls=%async_computation | async-start | bytes 4096 | tf_op jit(solution)/shard_map/all_to_all | solution.py:140
  9.5 0.8 %select_reduce_fusion.2 = (f32[32]{0:T(128)S(1)}, f32[32]{0:T(128)S(1)}) fusion(f32[8]{0:T(128)} %param.20, s32[32]{0:T(128)} %bitcast.133, f32[8]{0:T(128)} %param.21), kind=kLoop, calls=%fused_computation.238 | loop fusion | flops 1216 | bytes 448 | tf_op jit(solution)/shard_map/reduce_sum | solution.py:29
  10.3 0.8 %broadcast_multiply_fusion.1 = (f32[32,256]{1,0:T(8,128)S(1)}, f32[32,256]{1,0:T(8,128)S(1)}) fusion(f32[32]{0:T(128)S(1)} %get-tuple-element.2, f32[1,1,32,256]{3,2,1,0:T(8,128)} %param.15, f32[32]{0:T(128)S(1)} %get-tuple-element.3), kind=kLoop, calls=%fused_computation.226 | loop fusion | flops 16384 | bytes 98560 | tf_op jit(solution)/shard_map/mul | solution.py:120
  11.1 1.0 %fusion.130 = f32[48,768]{1,0:T(8,128)S(1)} fusion(f32[32,256]{1,0:T(8,128)S(1)} %get-tuple-element.30, f32[32,256]{1,0:T(8,128)S(1)} %get-tuple-element.29, f32[32,256]{1,0:T(8,128)} %bitcast.130, s32[32]{0:T(128)S(1)} %multiply_add_fusion.2, pred[32]{0:T(512)(128)(4,1)S(1)} %iota_compare_fusion.3), kind=kOutput, calls=%fused_computation.198 | convolution fusion | flops 14208000 | bytes 245920 | tf_op jit(solution)/shard_map/dot_general | solution.py:125
  12.1 0.7 reshape.99
  12.8 0.2 all-to-all-done
  13.0 3.5 %all-to-all-start.1 = ((f32[4,12,768]{2,1,0:T(8,128)}), f32[4,12,768]{2,1,0:T(8,128)S(1)}, u32[]{:S(2)}, u32[]{:S(2)}) async-start(f32[4,12,768]{2,1,0:T(8,128)} %reshape.99), calls=%async_computation.1 | async-start | bytes 393216 | tf_op jit(solution)/shard_map/all_to_all | solution.py:133
  16.5 0.1 sub.185
  16.5 3.9 %all-to-all-done.1 = f32[4,12,768]{2,1,0:T(8,128)S(1)} async-done(((f32[4,12,768]{2,1,0:T(8,128)}), f32[4,12,768]{2,1,0:T(8,128)S(1)}, u32[]{:S(2)}, u32[]{:S(2)}) %all-to-all-start.1) | async-done | bytes 147488 | tf_op jit(solution)/shard_map/all_to_all | solution.py:133
  20.5 0.5 fusion.126
  21.0 0.0 copy-done.2
  21.0 0.1 fusion.119
  21.1 0.0 copy-done
  21.2 2.7 %collective-permute-start = (f32[5,1,16,256]{3,2,1,0:T(8,128)S(1)}, f32[5,1,16,256]{3,2,1,0:T(8,128)S(1)}, u32[]{:S(2)}, u32[]{:S(2)}) collective-permute-start(f32[5,1,16,256]{3,2,1,0:T(8,128)S(1)} %get-tuple-element.23), channel_id=1, source_target_pairs={{0,8},{8,16},{16,24},{1,9},{9,17},{17,25},{2,10},{10,18},{18,26},{... | collective-permute-start | bytes 245768 | tf_op jit(solution)/shard_map/ppermute | solution.py:18
  23.9 1.3 %collective-permute-start.1 = (f32[5,1,16,256]{3,2,1,0:T(8,128)S(1)}, f32[5,1,16,256]{3,2,1,0:T(8,128)S(1)}, u32[]{:S(2)}, u32[]{:S(2)}) collective-permute-start(f32[5,1,16,256]{3,2,1,0:T(8,128)S(1)} %get-tuple-element.24), channel_id=1, source_target_pairs={{8,0},{16,8},{24,16},{9,1},{17,9},{25,17},{10,2},{18,10},{26,18},{... | collective-permute-start | bytes 245768 | tf_op jit(solution)/shard_map/ppermute | solution.py:20
  25.2 0.2 collective-permute-done
  25.3 3.7 %collective-permute-done.1 = f32[5,1,16,256]{3,2,1,0:T(8,128)S(1)} collective-permute-done((f32[5,1,16,256]{3,2,1,0:T(8,128)S(1)}, f32[5,1,16,256]{3,2,1,0:T(8,128)S(1)}, u32[]{:S(2)}, u32[]{:S(2)}) %collective-permute-start.1) | collective-permute-done | bytes 81952 | tf_op jit(solution)/shard_map/ppermute | solution.py:20
  29.1 0.1 pad_maximum_fusion.6
  29.2 7.6 %collective-permute-start.2 = (f32[5,18,1,256]{3,2,1,0:T(1,128)S(1)}, f32[5,18,1,256]{3,2,1,0:T(1,128)S(1)}, u32[]{:S(2)}, u32[]{:S(2)}) collective-permute-start(f32[5,18,1,256]{3,2,1,0:T(1,128)S(1)} %get-tuple-element.21), channel_id=1, source_target_pairs={{0,1},{1,2},{2,3},{3,4},{4,5},{5,6},{6,7},{8,9},{9,10},{10,11},{11... | collective-permute-start | bytes 276488 | tf_op jit(solution)/shard_map/ppermute | solution.py:18
  36.9 1.9 %collective-permute-start.3 = (f32[5,18,1,256]{3,2,1,0:T(1,128)S(1)}, f32[5,18,1,256]{3,2,1,0:T(1,128)S(1)}, u32[]{:S(2)}, u32[]{:S(2)}) collective-permute-start(f32[5,18,1,256]{3,2,1,0:T(1,128)S(1)} %get-tuple-element.22), channel_id=1, source_target_pairs={{1,0},{2,1},{3,2},{4,3},{5,4},{6,5},{7,6},{9,8},{10,9},{11,10},{12... | collective-permute-start | bytes 276488 | tf_op jit(solution)/shard_map/ppermute | solution.py:20
  38.8 0.0 collective-permute-done.2
  38.8 3.9 %collective-permute-done.3 = f32[5,18,1,256]{3,2,1,0:T(1,128)S(1)} collective-permute-done((f32[5,18,1,256]{3,2,1,0:T(1,128)S(1)}, f32[5,18,1,256]{3,2,1,0:T(1,128)S(1)}, u32[]{:S(2)}, u32[]{:S(2)}) %collective-permute-start.3) | collective-permute-done | bytes 92192 | tf_op jit(solution)/shard_map/ppermute | solution.py:20
  42.7 0.4 pad_maximum_fusion
  43.1 0.1 slice.352
  43.2 0.0 copy-start.1
  43.3 0.7 %fusion.3 = (f32[18,18,258]{2,1,0:T(8,128)S(1)}, f32[18,18,258]{2,1,0:T(8,128)S(1)}, f32[18,18,258]{2,1,0:T(8,128)S(1)}, f32[18,18,258]{2,1,0:T(8,128)S(1)}) fusion(f32[4,18,18,256]{3,2,1,0:T(8,128)S(1)} %slice.352), kind=kLoop, calls=%fused_computation.17 | loop fusion | bytes 2664576 | tf_op jit(solution)/shard_map/squeeze | solution.py:60
  44.0 0.1 maximum_bitcast_fusion
  44.1 0.4 copy-done.1
  44.5 0.8 %fusion.98 = (f32[1,16,16,256]{3,2,1,0:T(8,128)S(1)}, f32[16,16,256]{2,1,0:T(8,128)S(1)}, f32[16,16,256]{2,1,0:T(8,128)S(1)}, f32[16,16,256]{2,1,0:T(8,128)S(1)}...) fusion(f32[18,18,258]{2,1,0:T(8,128)S(1)} %get-tuple-element.18, ...), kind=kLoop, calls=%fused_computation.150 | loop fusion | flops 2621440 | bytes 6209536 | tf_op jit(solution)/shard_map/stack | solution.py:72
  45.3 0.5 fusion.122
  45.8 0.7 fusion.66
  46.5 0.7 fusion.82
  47.2 4.0 %collective-permute-start.4 = (f32[4,1,16,256]{3,2,1,0:T(8,128)S(1)}, f32[4,1,16,256]{3,2,1,0:T(8,128)S(1)}, u32[]{:S(2)}, u32[]{:S(2)}) collective-permute-start(f32[4,1,16,256]{3,2,1,0:T(8,128)S(1)} %get-tuple-element.27), channel_id=1, source_target_pairs={{0,8},{8,16},{16,24},{1,9},{9,17},{17,25},{2,10},{10,18},{18,26},{... | collective-permute-start | bytes 196616 | tf_op jit(solution)/shard_map/ppermute | solution.py:18
  51.2 1.3 %collective-permute-start.5 = (f32[4,1,16,256]{3,2,1,0:T(8,128)S(1)}, f32[4,1,16,256]{3,2,1,0:T(8,128)S(1)}, u32[]{:S(2)}, u32[]{:S(2)}) collective-permute-start(f32[4,1,16,256]{3,2,1,0:T(8,128)S(1)} %get-tuple-element.28), channel_id=1, source_target_pairs={{8,0},{16,8},{24,16},{9,1},{17,9},{25,17},{10,2},{18,10},{26,18},{... | collective-permute-start | bytes 196616 | tf_op jit(solution)/shard_map/ppermute | solution.py:20
  52.5 0.0 collective-permute-done.4
  52.5 3.7 %collective-permute-done.5 = f32[4,1,16,256]{3,2,1,0:T(8,128)S(1)} collective-permute-done((f32[4,1,16,256]{3,2,1,0:T(8,128)S(1)}, f32[4,1,16,256]{3,2,1,0:T(8,128)S(1)}, u32[]{:S(2)}, u32[]{:S(2)}) %collective-permute-start.5) | collective-permute-done | bytes 65568 | tf_op jit(solution)/shard_map/ppermute | solution.py:20
  56.2 0.1 pad_maximum_fusion.14
  56.3 3.4 %collective-permute-start.6 = (f32[4,18,1,256]{3,2,1,0:T(1,128)S(1)}, f32[4,18,1,256]{3,2,1,0:T(1,128)S(1)}, u32[]{:S(2)}, u32[]{:S(2)}) collective-permute-start(f32[4,18,1,256]{3,2,1,0:T(1,128)S(1)} %get-tuple-element.25), channel_id=1, source_target_pairs={{0,1},{1,2},{2,3},{3,4},{4,5},{5,6},{6,7},{8,9},{9,10},{10,11},{11... | collective-permute-start | bytes 221192 | tf_op jit(solution)/shard_map/ppermute | solution.py:18
  59.8 1.9 %collective-permute-start.7 = (f32[4,18,1,256]{3,2,1,0:T(1,128)S(1)}, f32[4,18,1,256]{3,2,1,0:T(1,128)S(1)}, u32[]{:S(2)}, u32[]{:S(2)}) collective-permute-start(f32[4,18,1,256]{3,2,1,0:T(1,128)S(1)} %get-tuple-element.26), channel_id=1, source_target_pairs={{1,0},{2,1},{3,2},{4,3},{5,4},{6,5},{7,6},{9,8},{10,9},{11,10},{12... | collective-permute-start | bytes 221192 | tf_op jit(solution)/shard_map/ppermute | solution.py:20
  61.7 0.0 collective-permute-done.6
  61.7 3.7 %collective-permute-done.7 = f32[4,18,1,256]{3,2,1,0:T(1,128)S(1)} collective-permute-done((f32[4,18,1,256]{3,2,1,0:T(1,128)S(1)}, f32[4,18,1,256]{3,2,1,0:T(1,128)S(1)}, u32[]{:S(2)}, u32[]{:S(2)}) %collective-permute-start.7) | collective-permute-done | bytes 73760 | tf_op jit(solution)/shard_map/ppermute | solution.py:20
  65.4 0.3 pad_maximum_fusion.1
  65.7 0.7 %fusion.7 = (f32[18,18,258]{2,1,0:T(8,128)S(1)}, f32[18,18,258]{2,1,0:T(8,128)S(1)}, f32[18,18,258]{2,1,0:T(8,128)S(1)}, f32[18,18,258]{2,1,0:T(8,128)S(1)}) fusion(f32[4,18,18,256]{3,2,1,0:T(8,128)S(1)} %pad_maximum_fusion.1), kind=kLoop, calls=%fused_computation.21 | loop fusion | bytes 2664576 | tf_op jit(solution)/shard_map/squeeze | solution.py:60
  66.5 0.7 fusion.50
  67.2 0.7 fusion.34
  67.9 0.0 copy-start.3
  67.9 0.5 fusion.125
  68.4 0.4 copy-done.3
  68.8 1.4 %fusion.14 = (f32[16,16,256]{2,1,0:T(8,128)}, f32[16,16,256]{2,1,0:T(8,128)S(1)}) fusion(f32[16,16,256]{2,1,0:T(8,128)S(1)} %copy-done.3, f32[16,16,3,256]{3,1,2,0:T(8,128)S(1)} %fusion.126, f32[16,16,256]{2,1,0:T(8,128)S(1)} %get-tuple-element.7, f32[16,16,256]{2,1,0:T(8,128)S(1)} %get-tuple-element.12, f32[16,16,256]{2,1,0:T(8,128)S(1)} %get-tuple-element.11, ...), kind=kLoop, calls=%fused_computation.30 | loop fusion | flops 2097152 | bytes 5505024 | tf_op jit(solution)/shard_map/mul | solution.py:162
  70.2 1.0 %pad_maximum_fusion.2 = f32[4,16,16,256]{3,2,1,0:T(8,128)} fusion(f32[1,16,16,256]{3,2,1,0:T(8,128)S(1)} %fusion.125, f32[1,16,16,256]{3,2,1,0:T(8,128)S(1)} %bitcast.128, f32[1,16,16,256]{3,2,1,0:T(8,128)S(1)} %fusion.34, f32[1,16,16,256]{3,2,1,0:T(8,128)S(1)} %fusion.50), kind=kLoop, calls=%fused_computation.11 | loop fusion | flops 786432 | bytes 2097152 | tf_op jit(solution)/shard_map/stack | solution.py:72
  (7 shorter events, 0.1 us)
Async XLA Ops:
  0.6 20.4 %copy-start.2 = (f32[16,16,256]{2,1,0:T(8,128)S(1)}, f32[16,16,256]{2,1,0:T(8,128)}, u32[]{:S(2)}) copy-start(f32[16,16,256]{2,1,0:T(8,128)} %param.13) | copy-start | bytes 786436
  0.6 20.5 %copy-start = (f32[4,16,16,256]{3,2,1,0:T(8,128)S(1)}, f32[4,16,16,256]{3,2,1,0:T(8,128)}, u32[]{:S(2)}) copy-start(f32[4,16,16,256]{3,2,1,0:T(8,128)} %param.11) | copy-start | bytes 3145732
  5.3 7.7 %all-to-all-start = ((f32[4,12,1]{1,2,0:T(1,128)}), f32[4,12,1]{1,2,0:T(1,128)S(1)}, u32[]{:S(2)}, u32[]{:S(2)}) async-start(f32[4,12,1]{1,2,0:T(1,128)} %convolution_bitcast_fusion), calls=%async_computation | async-start | bytes 4096 | tf_op jit(solution)/shard_map/all_to_all | solution.py:140
  13.0 7.5 %all-to-all-start.1 = ((f32[4,12,768]{2,1,0:T(8,128)}), f32[4,12,768]{2,1,0:T(8,128)S(1)}, u32[]{:S(2)}, u32[]{:S(2)}) async-start(f32[4,12,768]{2,1,0:T(8,128)} %reshape.99), calls=%async_computation.1 | async-start | bytes 393216 | tf_op jit(solution)/shard_map/all_to_all | solution.py:133
  21.2 4.2 %collective-permute-start = (f32[5,1,16,256]{3,2,1,0:T(8,128)S(1)}, f32[5,1,16,256]{3,2,1,0:T(8,128)S(1)}, u32[]{:S(2)}, u32[]{:S(2)}) collective-permute-start(f32[5,1,16,256]{3,2,1,0:T(8,128)S(1)} %get-tuple-element.23), channel_id=1, source_target_pairs={{0,8},{8,16},{16,24},{1,9},{9,17},{17,25},{2,10},{10,18},{18,26},{... | collective-permute-start | bytes 245768 | tf_op jit(solution)/shard_map/ppermute | solution.py:18
  23.9 5.2 %collective-permute-start.1 = (f32[5,1,16,256]{3,2,1,0:T(8,128)S(1)}, f32[5,1,16,256]{3,2,1,0:T(8,128)S(1)}, u32[]{:S(2)}, u32[]{:S(2)}) collective-permute-start(f32[5,1,16,256]{3,2,1,0:T(8,128)S(1)} %get-tuple-element.24), channel_id=1, source_target_pairs={{8,0},{16,8},{24,16},{9,1},{17,9},{25,17},{10,2},{18,10},{26,18},{... | collective-permute-start | bytes 245768 | tf_op jit(solution)/shard_map/ppermute | solution.py:20
  29.2 9.6 %collective-permute-start.2 = (f32[5,18,1,256]{3,2,1,0:T(1,128)S(1)}, f32[5,18,1,256]{3,2,1,0:T(1,128)S(1)}, u32[]{:S(2)}, u32[]{:S(2)}) collective-permute-start(f32[5,18,1,256]{3,2,1,0:T(1,128)S(1)} %get-tuple-element.21), channel_id=1, source_target_pairs={{0,1},{1,2},{2,3},{3,4},{4,5},{5,6},{6,7},{8,9},{9,10},{10,11},{11... | collective-permute-start | bytes 276488 | tf_op jit(solution)/shard_map/ppermute | solution.py:18
  36.9 5.9 %collective-permute-start.3 = (f32[5,18,1,256]{3,2,1,0:T(1,128)S(1)}, f32[5,18,1,256]{3,2,1,0:T(1,128)S(1)}, u32[]{:S(2)}, u32[]{:S(2)}) collective-permute-start(f32[5,18,1,256]{3,2,1,0:T(1,128)S(1)} %get-tuple-element.22), channel_id=1, source_target_pairs={{1,0},{2,1},{3,2},{4,3},{5,4},{6,5},{7,6},{9,8},{10,9},{11,10},{12... | collective-permute-start | bytes 276488 | tf_op jit(solution)/shard_map/ppermute | solution.py:20
  43.2 1.2 %copy-start.1 = (f32[4,16,16,256]{3,2,1,0:T(8,128)S(1)}, f32[4,16,16,256]{3,2,1,0:T(8,128)}, u32[]{:S(2)}) copy-start(f32[4,16,16,256]{3,2,1,0:T(8,128)} %param.12) | copy-start | bytes 3145732
  47.2 5.3 %collective-permute-start.4 = (f32[4,1,16,256]{3,2,1,0:T(8,128)S(1)}, f32[4,1,16,256]{3,2,1,0:T(8,128)S(1)}, u32[]{:S(2)}, u32[]{:S(2)}) collective-permute-start(f32[4,1,16,256]{3,2,1,0:T(8,128)S(1)} %get-tuple-element.27), channel_id=1, source_target_pairs={{0,8},{8,16},{16,24},{1,9},{9,17},{17,25},{2,10},{10,18},{18,26},{... | collective-permute-start | bytes 196616 | tf_op jit(solution)/shard_map/ppermute | solution.py:18
  51.2 5.0 %collective-permute-start.5 = (f32[4,1,16,256]{3,2,1,0:T(8,128)S(1)}, f32[4,1,16,256]{3,2,1,0:T(8,128)S(1)}, u32[]{:S(2)}, u32[]{:S(2)}) collective-permute-start(f32[4,1,16,256]{3,2,1,0:T(8,128)S(1)} %get-tuple-element.28), channel_id=1, source_target_pairs={{8,0},{16,8},{24,16},{9,1},{17,9},{25,17},{10,2},{18,10},{26,18},{... | collective-permute-start | bytes 196616 | tf_op jit(solution)/shard_map/ppermute | solution.py:20
  56.3 5.4 %collective-permute-start.6 = (f32[4,18,1,256]{3,2,1,0:T(1,128)S(1)}, f32[4,18,1,256]{3,2,1,0:T(1,128)S(1)}, u32[]{:S(2)}, u32[]{:S(2)}) collective-permute-start(f32[4,18,1,256]{3,2,1,0:T(1,128)S(1)} %get-tuple-element.25), channel_id=1, source_target_pairs={{0,1},{1,2},{2,3},{3,4},{4,5},{5,6},{6,7},{8,9},{9,10},{10,11},{11... | collective-permute-start | bytes 221192 | tf_op jit(solution)/shard_map/ppermute | solution.py:18
  59.8 5.7 %collective-permute-start.7 = (f32[4,18,1,256]{3,2,1,0:T(1,128)S(1)}, f32[4,18,1,256]{3,2,1,0:T(1,128)S(1)}, u32[]{:S(2)}, u32[]{:S(2)}) collective-permute-start(f32[4,18,1,256]{3,2,1,0:T(1,128)S(1)} %get-tuple-element.26), channel_id=1, source_target_pairs={{1,0},{2,1},{3,2},{4,3},{5,4},{6,5},{7,6},{9,8},{10,9},{11,10},{12... | collective-permute-start | bytes 221192 | tf_op jit(solution)/shard_map/ppermute | solution.py:20
  67.9 1.0 %copy-start.3 = (f32[16,16,256]{2,1,0:T(8,128)S(1)}, f32[16,16,256]{2,1,0:T(8,128)}, u32[]{:S(2)}) copy-start(f32[16,16,256]{2,1,0:T(8,128)} %param.14) | copy-start | bytes 786436
where the time goes:
time: 71.9 us; the launch traced here: 71.2 us
  starting transfers between devices  31.9 us (44%)
  waiting for transfers between devices  19.4 us (27%)
  other arithmetic  12.1 us (17%)
  local copies, waits for them, and re-layouts  3.22 us (4%)
  matrix products  3.01 us (4%)
  between operations  1.63 us (2%)
    ppermute x4, starting transfers between devices, with_halo(): lax.ppermute(tail, axis, [(i, (i + 1) % count) for i in range(ends)])  17.8 us
    ppermute x4, waiting for transfers between devices, with_halo(): lax.ppermute(head, axis, [((i + 1) % count, i) for i in range(ends)])  15.1 us
    ppermute x4, starting transfers between devices, with_halo(): lax.ppermute(head, axis, [((i + 1) % count, i) for i in range(ends)])  6.43 us
    another operation x8, other arithmetic, smooth_once(): return jnp.stack(results)  5.64 us
    all_to_all x1, starting transfers between devices, on_device(): lax.all_to_all(sent_meta.reshape(owners, capacity, 1), 'gx', split_axis=0...  4.25 us
    all_to_all x1, waiting for transfers between devices, on_device(): lax.all_to_all(sent_rows.reshape(owners, capacity, 3 * depth), 'gx', spli...  3.94 us
    all_to_all x1, starting transfers between devices, on_device(): lax.all_to_all(sent_rows.reshape(owners, capacity, 3 * depth), 'gx', spli...  3.48 us
    dot_general x1, matrix products, on_device(): jnp.dot(selector, (columns + 1).astype(jnp.float32)[:, None], precision=h...  1.53 us
  transfers between devices with their start and end apart: 10, of which 7 were waited for; matrix products, arithmetic and copies ran while one was open for 5% of the time, Pallas kernels for 0%

commit v1 on v0

v1 whole, which is shorter than its diff:
```python
import functools

import jax
import jax.numpy as jnp
from jax import lax
from jax.experimental import pallas as pl
from jax.experimental.pallas import tpu as pltpu
from jax.sharding import PartitionSpec as P

RELAX_VELOCITY = 0.6
RELAX_PRESSURE = 0.5
MESH = pl.DeviceIdType.MESH


def kernel(
    n,
    m,
    start_h,
    source_h,
    bglog_h,
    bgden_h,
    weights_h,
    phase_ref,
    owner_ref,
    column_ref,
    active_ref,
    table_log,
    table_den,
    out_ref,
    sens_ref,
    f0,
    f1,
    src,
    bg,
    bd,
    visc,
    dens,
    cx,
    cyu,
    cyl,
    czu,
    czl,
    rec,
    sums,
    wb,
    mraw,
    mb,
    ys,
    yr,
    ysv,
    yrv,
    ys2,
    yr2,
    local_sem,
    w_send,
    w_recv,
    m_send,
    m_recv,
    h_send,
    h_recv,
):
    X, Y, Z = bd.shape
    B = weights_h.shape[2]
    W = mraw.shape[1]
    rows = wb.shape[0]
    a = lax.axis_index("gx")
    b = lax.axis_index("gy")
    has_xlo, has_xhi = a > 0, a < n - 1
    has_ylo, has_yhi = b > 0, b < m - 1

    own_w = pltpu.make_async_copy(
        weights_h.at[0, 0], wb.at[pl.ds(pl.multiple_of(a * B, B), B)], local_sem.at[0]
    )
    own_start = pltpu.make_async_copy(start_h, f0.at[:, pl.ds(1, X)], local_sem.at[1])
    own_bg = pltpu.make_async_copy(bglog_h, bg.at[pl.ds(1, X)], local_sem.at[2])
    own_bd = pltpu.make_async_copy(bgden_h, bd, local_sem.at[3])
    own_src = pltpu.make_async_copy(source_h, src, local_sem.at[4])
    own_start.start()
    own_w.start()
    own_bg.start()
    own_bd.start()
    own_src.start()

    barrier = pltpu.get_barrier_semaphore()
    for s in range(1, n):
        pl.semaphore_signal(
            barrier, inc=1, device_id=(lax.rem(a + s, n), b), device_id_type=MESH
        )

    @pl.when(has_ylo)
    def _():
        pl.semaphore_signal(barrier, inc=1, device_id=(a, b - 1), device_id_type=MESH)

    @pl.when(has_yhi)
    def _():
        pl.semaphore_signal(barrier, inc=1, device_id=(a, b + 1), device_id_type=MESH)

    phase = phase_ref[0]
    lane = lax.broadcasted_iota(jnp.int32, (1, B), 1)
    live = lane < active_ref[0, 0]
    code = jnp.where(live, owner_ref[0] * (X * Y) + column_ref[0], -2 * X * Y)
    log_value = jnp.zeros((1, B), jnp.float32)
    den_value = jnp.zeros((1, B), jnp.float32)
    for k in range(table_log.shape[0]):
        log_value = jnp.where(phase == k, table_log[k], log_value)
        den_value = jnp.where(phase == k, table_den[k], den_value)
    mraw[...] = jnp.zeros_like(mraw)
    mraw[0:1, 0:B] = code.astype(jnp.float32)
    mraw[1:2, 0:B] = log_value
    mraw[2:3, 0:B] = den_value
    mb[0] = pltpu.roll(mraw[...], a * B, 1)

    @pl.when(a == 0)
    def _():
        f0[:, 0] = jnp.zeros((4, Y, Z), jnp.float32)
        f1[:, 0] = jnp.zeros((4, Y, Z), jnp.float32)
        bg[0] = jnp.zeros((Y, Z), jnp.float32)

    @pl.when(a == n - 1)
    def _():
        f0[:, X + 1] = jnp.zeros((4, Y, Z), jnp.float32)
        f1[:, X + 1] = jnp.zeros((4, Y, Z), jnp.float32)
        bg[X + 1] = jnp.zeros((Y, Z), jnp.float32)

    @pl.when(b == 0)
    def _():
        yr[0] = jnp.zeros((4, X, Z), jnp.float32)
        yr2[0] = jnp.zeros((4, X, Z), jnp.float32)
        yrv[0] = jnp.zeros((X, Z), jnp.float32)

    @pl.when(b == m - 1)
    def _():
        yr[1] = jnp.zeros((4, X, Z), jnp.float32)
        yr2[1] = jnp.zeros((4, X, Z), jnp.float32)
        yrv[1] = jnp.zeros((X, Z), jnp.float32)

    pl.semaphore_wait(
        barrier, n - 1 + has_ylo.astype(jnp.int32) + has_yhi.astype(jnp.int32)
    )

    def remote(source, target, slot, peer):
        return pltpu.make_async_remote_copy(
            src_ref=source,
            dst_ref=target,
            send_sem=h_send.at[slot],
            recv_sem=h_recv.at[slot],
            device_id=peer,
            device_id_type=MESH,
        )

    w_copies, m_copies = [], []
    for s in range(1, n):
        peer = (lax.rem(a + s, n), b)
        m_copies.append(
            pltpu.make_async_remote_copy(
                mb.at[0], mb.at[s], m_send.at[s], m_recv.at[s], peer, MESH
            )
        )
        w_copies.append(
            pltpu.make_async_remote_copy(
                weights_h.at[0, 0],
                wb.at[pl.ds(pl.multiple_of(a * B, B), B)],
                w_send.at[s],
                w_recv.at[s],
                peer,
                MESH,
            )
        )
        w_copies[-1].start()
        m_copies[-1].start()

    lo_x, hi_x, lo_y, hi_y = (a - 1, b), (a + 1, b), (a, b - 1), (a, b + 1)
    pairs = {
        "bg": (
            remote(bglog_h.at[0], bg.at[X + 1], 0, lo_x),
            remote(bglog_h.at[X - 1], bg.at[0], 1, hi_x),
            has_xlo,
            has_xhi,
        ),
        "x0": (
            remote(start_h.at[:, 0], f0.at[:, X + 1], 2, lo_x),
            remote(start_h.at[pl.ds(0, 3), X - 1], f0.at[pl.ds(0, 3), 0], 3, hi_x),
            has_xlo,
            has_xhi,
        ),
        "y0": (
            remote(ys.at[0], yr.at[1], 4, lo_y),
            remote(ys.at[1, pl.ds(0, 3)], yr.at[0, pl.ds(0, 3)], 5, hi_y),
            has_ylo,
            has_yhi,
        ),
        "yv": (
            remote(ysv.at[0], yrv.at[1], 6, lo_y),
            remote(ysv.at[1], yrv.at[0], 7, hi_y),
            has_ylo,
            has_yhi,
        ),
        "x1": (
            remote(f1.at[:, 1], f1.at[:, X + 1], 8, lo_x),
            remote(f1.at[pl.ds(0, 3), X], f1.at[pl.ds(0, 3), 0], 9, hi_x),
            has_xlo,
            has_xhi,
        ),
        "y1": (
            remote(ys2.at[0], yr2.at[1], 10, lo_y),
            remote(ys2.at[1, pl.ds(0, 3)], yr2.at[0, pl.ds(0, 3)], 11, hi_y),
            has_ylo,
            has_yhi,
        ),
    }

    def launch_down(name):
        down, up, lo, hi = pairs[name]
        pl.when(lo)(down.start)

    def launch_up(name):
        down, up, lo, hi = pairs[name]
        pl.when(hi)(up.start)

    def arrive(name):
        down, up, lo, hi = pairs[name]
        pl.when(hi)(down.wait_recv)
        pl.when(lo)(up.wait_recv)

    def sent(name):
        down, up, lo, hi = pairs[name]
        pl.when(lo)(down.wait_send)
        pl.when(hi)(up.wait_send)

    launch_down("bg")
    launch_up("bg")
    launch_down("x0")
    launch_up("x0")

    own_start.wait()
    for c in range(4):
        for x in range(X):
            ys[0, c, x : x + 1, :] = f0[c, x + 1, 0:1, :]
            if c < 3:
                ys[1, c, x : x + 1, :] = f0[c, x + 1, Y - 1 : Y, :]
    launch_down("y0")
    launch_up("y0")

    own_w.wait()
    own_bg.wait()
    own_bd.wait()
    for s in range(1, n):
        m_copies[s - 1].wait_recv()
        w_copies[s - 1].wait_recv()

    meta = mb[0]
    for s in range(1, n):
        meta = meta + mb[s]
    columns = meta.T
    weights = wb[...]
    payload = jnp.concatenate(
        [weights, weights * columns[:rows, 1:2], weights * columns[:rows, 2:3]], axis=1
    )
    coarse = payload.astype(jnp.bfloat16)
    fine = (payload - coarse.astype(jnp.float32)).astype(jnp.bfloat16)
    cells = (X + 2) * Y
    ids = lax.broadcasted_iota(jnp.int32, (cells, rows), 0) + (a * (X * Y) - Y)
    hot = (ids.astype(jnp.float32) == meta[0:1, :rows]).astype(jnp.float32).astype(jnp.bfloat16)
    sums[...] = jnp.dot(hot, coarse, preferred_element_type=jnp.float32) + jnp.dot(
        hot, fine, preferred_element_type=jnp.float32
    )

    arrive("bg")
    for i in range(X + 2):
        part = sums[i * Y : (i + 1) * Y, :]
        scale = 1.0 / (1.0 + part[:, :Z])
        value = jnp.exp((bg[i] + part[:, Z : 2 * Z]) * scale)
        if i == 0:
            value = jnp.where(has_xlo, value, 0.0)
        elif i == X + 1:
            value = jnp.where(has_xhi, value, 0.0)
        else:
            dens[i - 1] = (bd[i - 1] + part[:, 2 * Z :]) * scale
            ysv[0, i - 1 : i, :] = value[0:1, :]
            ysv[1, i - 1 : i, :] = value[Y - 1 : Y, :]
        visc[i] = value
    launch_down("yv")
    launch_up("yv")

    row_id = lax.broadcasted_iota(jnp.int32, (Y, Z), 0)
    lane_id = lax.broadcasted_iota(jnp.int32, (Y, Z), 1)
    first_row, last_row = row_id == 0, row_id == Y - 1
    first_lane, last_lane = lane_id == 0, lane_id == Z - 1

    def y_next(plane, halo):
        return jnp.where(last_row, halo, pltpu.roll(plane, Y - 1, 0))

    def y_prev(plane, halo):
        return jnp.where(first_row, halo, pltpu.roll(plane, 1, 0))

    def z_next(plane):
        return pltpu.roll(plane, Z - 1, 1)

    def z_prev(plane):
        return pltpu.roll(plane, 1, 1)

    for i in range(X + 1):
        cx[i] = 0.5 * (visc[i] + visc[i + 1])

    own_src.wait()
    arrive("yv")
    for x in range(X):
        v = visc[x + 1]
        half = 0.5 * v
        y_up = 0.5 * (v + y_next(v, yrv[1, x : x + 1, :]))
        y_down = 0.5 * (v + y_prev(v, yrv[0, x : x + 1, :]))
        z_up = jnp.where(last_lane, 0.0, 0.5 * (v + z_next(v)))
        z_down = z_prev(z_up)
        edge = jnp.where(first_lane | last_lane, half, 0.0)
        diagonal = cx[x] + cx[x + 1] + y_up + y_down + z_up + z_down + edge
        cyu[x] = y_up
        cyl[x] = y_down
        czu[x] = z_up
        czl[x] = z_down
        rec[x] = RELAX_VELOCITY / diagonal
    arrive("y0")
    arrive("x0")

    def sweep(field, halo, x):
        i = x + 1
        press = field[3, i]
        scale = rec[x]
        divergence = src[3, x]
        results = []
        for c in range(3):
            u = field[c, i]
            below_x = field[c, i - 1]
            below_y = y_prev(u, halo[0, c, x : x + 1, :])
            below_z = z_prev(u)
            total = cx[i] * field[c, i + 1] + cx[i - 1] * below_x
            total = total + cyu[x] * y_next(u, halo[1, c, x : x + 1, :]) + cyl[x] * below_y
            total = total + czu[x] * z_next(u) + czl[x] * below_z
            if c == 0:
                ahead, behind = field[3, i + 1], below_x
            elif c == 1:
                ahead, behind = y_next(press, halo[1, 3, x : x + 1, :]), below_y
            else:
                ahead = jnp.where(last_lane, 0.0, z_next(press))
                behind = jnp.where(first_lane, 0.0, below_z)
            residual = src[c, x] + total - (ahead - press)
            results.append((1.0 - RELAX_VELOCITY) * u + scale * residual)
            divergence = divergence + (u - behind)
        results.append(press - RELAX_PRESSURE * visc[i] * divergence)
        return results

    def first(x):
        for c, plane in enumerate(sweep(f0, yr, x)):
            f1[c, x + 1] = plane
            ys2[0, c, x : x + 1, :] = plane[0:1, :]
            if c < 3:
                ys2[1, c, x : x + 1, :] = plane[Y - 1 : Y, :]

    first(0)
    launch_down("x1")
    first(X - 1)
    launch_up("x1")
    for x in range(1, X - 1):
        first(x)
    launch_down("y1")
    launch_up("y1")
    arrive("y1")

    def second(x):
        planes = sweep(f1, yr2, x)
        for c, plane in enumerate(planes):
            out_ref[c, x] = plane
        sens_ref[x] = dens[x] * planes[2]

    for x in range(1, X - 1):
        second(x)
    arrive("x1")
    second(0)
    second(X - 1)

    for copy in w_copies + m_copies:
        copy.wait_send()
    for name in pairs:
        sent(name)


def on_device(n, m, *arrays):
    start, weights = arrays[0], arrays[4]
    _, X, Y, Z = start.shape
    B = weights.shape[2]
    rows = n * B
    W = -(-rows // 128) * 128
    f32 = jnp.float32
    vmem = pl.BlockSpec(memory_space=pltpu.VMEM)
    smem = pl.BlockSpec(memory_space=pltpu.SMEM)
    anywhere = pl.BlockSpec(memory_space=pl.ANY)
    block = pltpu.VMEM((X, Y, Z), f32)
    padded = pltpu.VMEM((X + 2, Y, Z), f32)
    faces = pltpu.VMEM((2, 4, X, Z), f32)
    face = pltpu.VMEM((2, X, Z), f32)
    dma = pltpu.SemaphoreType.DMA
    return pl.pallas_call(
        functools.partial(kernel, n, m),
        out_shape=(
            jax.ShapeDtypeStruct((4, X, Y, Z), f32),
            jax.ShapeDtypeStruct((X, Y, Z), f32),
        ),
        in_specs=[anywhere] * 5 + [vmem] * 3 + [smem] * 3,
        out_specs=(vmem, vmem),
        scratch_shapes=[
            pltpu.VMEM((4, X + 2, Y, Z), f32),
            pltpu.VMEM((4, X + 2, Y, Z), f32),
            pltpu.VMEM((4, X, Y, Z), f32),
            padded,
            block,
            padded,
            block,
            pltpu.VMEM((X + 1, Y, Z), f32),
            block,
            block,
            block,
            block,
            block,
            pltpu.VMEM(((X + 2) * Y, 3 * Z), f32),
            pltpu.VMEM((rows, Z), f32),
            pltpu.VMEM((8, W), f32),
            pltpu.VMEM((n, 8, W), f32),
            faces,
            faces,
            face,
            face,
            faces,
            faces,
            dma((5,)),
            dma((n,)),
            dma((n,)),
            dma((n,)),
            dma((n,)),
            dma((12,)),
            dma((12,)),
        ],
        compiler_params=pltpu.CompilerParams(
            collective_id=0, has_side_effects=True, vmem_limit_bytes=40 * 1024 * 1024
        ),
    )(*arrays)


def solution(mesh):
    in_specs = (
        P(None, "gx", "gy", None),
        P(None, "gx", "gy", None),
        P("gx", "gy", None),
        P("gx", "gy", None),
        P("gx", "gy", None, None),
        P("gx", "gy", None),
        P("gx", "gy", None),
        P("gx", "gy", None),
        P("gx", "gy"),
        P(),
        P(),
    )
    out_specs = (P(None, "gx", "gy", None), P("gx", "gy", None))
    return jax.shard_map(
        functools.partial(on_device, mesh.shape["gx"], mesh.shape["gy"]),
        mesh=mesh,
        in_specs=in_specs,
        out_specs=out_specs,
        check_vma=False,
    )
```

time: 71.9 us -> 25.7 us (0.36)
  starting transfers between devices: 31.9 us -> 0 us
  waiting for transfers between devices: 19.4 us -> 0 us
  Pallas kernels: 0 us -> 15.8 us
  other arithmetic: 12.1 us -> 0 us
  local copies, waits for them, and re-layouts: 3.22 us -> 8.1 us
  matrix products: 3.01 us -> 0 us
    ppermute x8 -> x0, starting transfers between devices: 24.2 us -> none  [the longest x4 17.8 us: with_halo(): lax.ppermute(tail, axis, [(i, (i + 1) % count) for i in range(ends)])]
    pallas_call x0 -> x1, Pallas kernels: none -> 15.8 us  [on_device(): pl.pallas_call(functools.partial(kernel, n, m), out_shape=(jax.ShapeDtype...]
    ppermute x8 -> x0, waiting for transfers between devices: 15.3 us -> none  [the longest x4 15.1 us: with_halo(): lax.ppermute(head, axis, [((i + 1) % count, i) for i in range(ends)])]
    all_to_all x2 -> x0, starting transfers between devices: 7.73 us -> none  [the longest x1 4.25 us: on_device(): lax.all_to_all(sent_meta.reshape(owners, capacity, 1), 'gx', split_axis=0...]
    unnamed x8 -> x22, local copies, waits for them, and re-layouts: 0.8 us -> 8.1 us
    another operation x9 -> x0, other arithmetic: 5.7 us -> none  [the longest x8 5.64 us: smooth_once(): return jnp.stack(results)]
    all_to_all x2 -> x0, waiting for transfers between devices: 4.1 us -> none  [the longest x1 3.94 us: on_device(): lax.all_to_all(sent_rows.reshape(owners, capacity, 3 * depth), 'gx', spli...]
    dot_general x3 -> x0, matrix products: 3.01 us -> none  [the longest x1 1.53 us: on_device(): jnp.dot(selector, (columns + 1).astype(jnp.float32)[:, None], precision=h...]
  transfers between devices with their start and end apart: 10 -> 0, of which waited for: 7 -> 0; matrix products, arithmetic and copies ran while one was open for 5% -> 0% of each run, Pallas kernels for 0% -> 0%
where the time goes in v1:
time: 25.7 us; the launch traced here: 25.3 us
  Pallas kernels  15.8 us (61%)
  local copies, waits for them, and re-layouts  8.1 us (32%)
  between operations  1.37 us (5%)
    pallas_call x1, Pallas kernels, on_device(): pl.pallas_call(functools.partial(kernel, n, m), out_shape=(jax.ShapeDtype...  15.8 us
    unnamed x22, local copies, waits for them, and re-layouts  8.1 us

profile of v1, /device:TPU:1, one launch (start us, length us, event | category | flops | bytes accessed | tf_op | source)
XLA Modules:
  0.0 25.3 jit_solution(14449627258709311518)
XLA Ops:
  0.6 0.0 copy-start.7
  0.6 0.0 copy-start.6
  0.7 0.0 copy-start.5
  1.3 0.0 copy-done.7
  1.3 0.0 copy-done.6
  1.4 0.0 copy-done.5
  1.4 0.0 copy-start
  1.4 1.2 %copy-done = f32[4,16,16,256]{3,2,1,0:T(8,128)S(1)} copy-done((f32[4,16,16,256]{3,2,1,0:T(8,128)S(1)}, f32[4,16,16,256]{3,2,1,0:T(8,128)}, u32[]{:S(2)}) %copy-start) | copy-done | bytes 1048600
  2.6 0.0 copy-start.1
  2.6 1.2 %copy-done.1 = f32[4,16,16,256]{3,2,1,0:T(8,128)S(1)} copy-done((f32[4,16,16,256]{3,2,1,0:T(8,128)S(1)}, f32[4,16,16,256]{3,2,1,0:T(8,128)}, u32[]{:S(2)}) %copy-start.1) | copy-done | bytes 1048600
  3.8 0.0 copy-start.2
  3.8 0.9 %copy-done.2 = f32[16,16,256]{2,1,0:T(8,128)S(1)} copy-done((f32[16,16,256]{2,1,0:T(8,128)S(1)}, f32[16,16,256]{2,1,0:T(8,128)}, u32[]{:S(2)}) %copy-start.2) | copy-done | bytes 262168
  4.8 0.0 copy-start.3
  4.8 0.9 %copy-done.3 = f32[16,16,256]{2,1,0:T(8,128)S(1)} copy-done((f32[16,16,256]{2,1,0:T(8,128)S(1)}, f32[16,16,256]{2,1,0:T(8,128)}, u32[]{:S(2)}) %copy-start.3) | copy-done | bytes 262168
  5.7 0.0 copy-start.4
  5.7 0.8 %copy-done.4 = f32[1,1,32,256]{3,2,1,0:T(8,128)S(1)} copy-done((f32[1,1,32,256]{3,2,1,0:T(8,128)S(1)}, f32[1,1,32,256]{3,2,1,0:T(8,128)}, u32[]{:S(2)}) %copy-start.4) | copy-done | bytes 32792
  6.5 0.0 copy-start.8
  6.5 0.7 %copy-done.8 = f32[8]{0:T(128)S(1)} copy-done((f32[8]{0:T(128)S(1)}, f32[8]{0:T(128)}, u32[]{:S(2)}) %copy-start.8) | copy-done | bytes 56
  7.1 0.0 copy-start.9
  7.1 0.7 %copy-done.9 = f32[8]{0:T(128)S(1)} copy-done((f32[8]{0:T(128)S(1)}, f32[8]{0:T(128)}, u32[]{:S(2)}) %copy-start.9) | copy-done | bytes 56
  7.8 15.8 %shard_map.122 = (f32[4,16,16,256]{3,2,1,0:T(8,128)S(1)}, f32[16,16,256]{2,1,0:T(8,128)S(1)}) custom-call(f32[4,16,16,256]{3,2,1,0:T(8,128)S(1)} %copy-done, f32[4,16,16,256]{3,2,1,0:T(8,128)S(1)} %copy-done.1, f32[16,16,256]{2,1,0:T(8,128)S(1)} %copy-done.2, f32[16,16,256]{2,1,0:T(8,128)S(1)} %copy-done.3, f32[1,1,32,256]{3,2,1,0:T(8,128)S(1)} %copy-done.4, ...), custom_call_target="tpu_custom_call" | custom-call | tf_op jit(solution)/shard_map/pallas_call | solution.py:401
  23.6 1.0 %copy.16 = f32[4,16,16,256]{3,2,1,0:T(8,128)} copy(f32[4,16,16,256]{3,2,1,0:T(8,128)S(1)} %get-tuple-element.4) | data formatting | bytes 2097152
  24.6 0.7 %copy.17 = f32[16,16,256]{2,1,0:T(8,128)} copy(f32[16,16,256]{2,1,0:T(8,128)S(1)} %get-tuple-element.5) | data formatting | bytes 524288
Async XLA Ops:
  0.6 0.7 %copy-start.7 = (s32[1,1,32]{2,1,0:T(1,128)S(1)}, s32[1,1,32]{2,1,0:T(1,128)}, u32[]{:S(2)}) copy-start(s32[1,1,32]{2,1,0:T(1,128)} %column_ref.1) | copy-start | bytes 388
  0.6 0.7 %copy-start.6 = (s32[1,1,32]{2,1,0:T(1,128)S(1)}, s32[1,1,32]{2,1,0:T(1,128)}, u32[]{:S(2)}) copy-start(s32[1,1,32]{2,1,0:T(1,128)} %owner_ref.1) | copy-start | bytes 388
  0.7 0.7 %copy-start.5 = (s32[1,1,32]{2,1,0:T(1,128)S(1)}, s32[1,1,32]{2,1,0:T(1,128)}, u32[]{:S(2)}) copy-start(s32[1,1,32]{2,1,0:T(1,128)} %phase_ref.1) | copy-start | bytes 388
  1.4 1.2 %copy-start = (f32[4,16,16,256]{3,2,1,0:T(8,128)S(1)}, f32[4,16,16,256]{3,2,1,0:T(8,128)}, u32[]{:S(2)}) copy-start(f32[4,16,16,256]{3,2,1,0:T(8,128)} %start_h.1) | copy-start | bytes 3145732
  2.6 1.2 %copy-start.1 = (f32[4,16,16,256]{3,2,1,0:T(8,128)S(1)}, f32[4,16,16,256]{3,2,1,0:T(8,128)}, u32[]{:S(2)}) copy-start(f32[4,16,16,256]{3,2,1,0:T(8,128)} %source_h.1) | copy-start | bytes 3145732
  3.8 0.9 %copy-start.2 = (f32[16,16,256]{2,1,0:T(8,128)S(1)}, f32[16,16,256]{2,1,0:T(8,128)}, u32[]{:S(2)}) copy-start(f32[16,16,256]{2,1,0:T(8,128)} %bglog_h.1) | copy-start | bytes 786436
  4.8 0.9 %copy-start.3 = (f32[16,16,256]{2,1,0:T(8,128)S(1)}, f32[16,16,256]{2,1,0:T(8,128)}, u32[]{:S(2)}) copy-start(f32[16,16,256]{2,1,0:T(8,128)} %bgden_h.1) | copy-start | bytes 786436
  5.7 0.8 %copy-start.4 = (f32[1,1,32,256]{3,2,1,0:T(8,128)S(1)}, f32[1,1,32,256]{3,2,1,0:T(8,128)}, u32[]{:S(2)}) copy-start(f32[1,1,32,256]{3,2,1,0:T(8,128)} %weights_h.1) | copy-start | bytes 98308
  6.5 0.7 %copy-start.8 = (f32[8]{0:T(128)S(1)}, f32[8]{0:T(128)}, u32[]{:S(2)}) copy-start(f32[8]{0:T(128)} %table_log.1) | copy-start | bytes 100
  7.1 0.7 %copy-start.9 = (f32[8]{0:T(128)S(1)}, f32[8]{0:T(128)}, u32[]{:S(2)}) copy-start(f32[8]{0:T(128)} %table_den.1) | copy-start | bytes 100

commit v2 on v1

--- a/solution.py
+++ b/solution.py
@@ -20,12 +20,12 @@
     bglog_h,
     bgden_h,
     weights_h,
-    phase_ref,
-    owner_ref,
-    column_ref,
+    phase_h,
+    owner_h,
+    column_h,
     active_ref,
-    table_log,
-    table_den,
+    table_log_h,
+    table_den_h,
     out_ref,
     sens_ref,
     f0,
@@ -51,6 +51,19 @@
     yrv,
     ys2,
     yr2,
+    fin,
+    fin2,
+    fsrc,
+    vin,
+    fc,
+    xs,
+    xrs,
+    xr,
+    phase_ref,
+    owner_ref,
+    column_ref,
+    table_log,
+    table_den,
     local_sem,
     w_send,
     w_recv,
@@ -68,6 +81,34 @@
     has_xlo, has_xhi = a > 0, a < n - 1
     has_ylo, has_yhi = b > 0, b < m - 1
 
+    barrier = pltpu.get_barrier_semaphore()
+    for s in range(1, n):
+        pl.semaphore_signal(
+            barrier, inc=1, device_id=(lax.rem(a + s, n), b), device_id_type=MESH
+        )
+
+    @pl.when(has_ylo)
+    def _():
+        pl.semaphore_signal(barrier, inc=1, device_id=(a, b - 1), device_id_type=MESH)
+
+    @pl.when(has_yhi)
+    def _():
+        pl.semaphore_signal(barrier, inc=1, device_id=(a, b + 1), device_id_type=MESH)
+
+    small = [
+        pltpu.make_async_copy(source, target, local_sem.at[5 + k])
+        for k, (source, target) in enumerate(
+            [
+                (phase_h, phase_ref),
+                (owner_h, owner_ref),
+                (column_h, column_ref),
+                (table_log_h, table_log),
+                (table_den_h, table_den),
+            ]
+        )
+    ]
+    for copy in small:
+        copy.start()
     own_w = pltpu.make_async_copy(
         weights_h.at[0, 0], wb.at[pl.ds(pl.multiple_of(a * B, B), B)], local_sem.at[0]
     )
@@ -81,19 +122,8 @@
     own_bd.start()
     own_src.start()
 
-    barrier = pltpu.get_barrier_semaphore()
-    for s in range(1, n):
-        pl.semaphore_signal(
-            barrier, inc=1, device_id=(lax.rem(a + s, n), b), device_id_type=MESH
-        )
-
-    @pl.when(has_ylo)
-    def _():
-        pl.semaphore_signal(barrier, inc=1, device_id=(a, b - 1), device_id_type=MESH)
-
-    @pl.when(has_yhi)
-    def _():
-        pl.semaphore_signal(barrier, inc=1, device_id=(a, b + 1), device_id_type=MESH)
+    for copy in small:
+        copy.wait()
 
     phase = phase_ref[0]
     lane = lax.broadcasted_iota(jnp.int32, (1, B), 1)
@@ -115,12 +145,14 @@
         f0[:, 0] = jnp.zeros((4, Y, Z), jnp.float32)
         f1[:, 0] = jnp.zeros((4, Y, Z), jnp.float32)
         bg[0] = jnp.zeros((Y, Z), jnp.float32)
+        xr[0] = jnp.zeros((8, Z), jnp.float32)
 
     @pl.when(a == n - 1)
     def _():
         f0[:, X + 1] = jnp.zeros((4, Y, Z), jnp.float32)
         f1[:, X + 1] = jnp.zeros((4, Y, Z), jnp.float32)
         bg[X + 1] = jnp.zeros((Y, Z), jnp.float32)
+        xr[1] = jnp.zeros((8, Z), jnp.float32)
 
     @pl.when(b == 0)
     def _():
@@ -196,8 +228,8 @@
             has_yhi,
         ),
         "x1": (
-            remote(f1.at[:, 1], f1.at[:, X + 1], 8, lo_x),
-            remote(f1.at[pl.ds(0, 3), X], f1.at[pl.ds(0, 3), 0], 9, hi_x),
+            remote(xs.at[0], f1.at[:, X + 1], 8, lo_x),
+            remote(xs.at[1, pl.ds(0, 3)], f1.at[pl.ds(0, 3), 0], 9, hi_x),
             has_xlo,
             has_xhi,
         ),
@@ -208,6 +240,13 @@
             has_yhi,
         ),
     }
+
+    pairs["xr"] = (
+        remote(xrs.at[0], xr.at[1], 12, lo_x),
+        remote(xrs.at[1], xr.at[0], 13, hi_x),
+        has_xlo,
+        has_xhi,
+    )
 
     def launch_down(name):
         down, up, lo, hi = pairs[name]
@@ -240,6 +279,19 @@
                 ys[1, c, x : x + 1, :] = f0[c, x + 1, Y - 1 : Y, :]
     launch_down("y0")
     launch_up("y0")
+    edges = (0, Y - 1)
+    inners = (1, Y - 2)
+    for side in range(2):
+        for c in range(4):
+            for x in range(X):
+                fin[side, c, x : x + 1, :] = f0[c, x + 1, inners[side] : inners[side] + 1, :]
+                if side == 1 and c == 3:
+                    ys[1, c, x : x + 1, :] = f0[c, x + 1, Y - 1 : Y, :]
+    own_src.wait()
+    for side in range(2):
+        for c in range(4):
+            for x in range(X):
+                fsrc[side, c, x : x + 1, :] = src[c, x, edges[side] : edges[side] + 1, :]
 
     own_w.wait()
     own_bg.wait()
@@ -278,19 +330,27 @@
             dens[i - 1] = (bd[i - 1] + part[:, 2 * Z :]) * scale
             ysv[0, i - 1 : i, :] = value[0:1, :]
             ysv[1, i - 1 : i, :] = value[Y - 1 : Y, :]
+            vin[0, i - 1 : i, :] = value[1:2, :]
+            vin[1, i - 1 : i, :] = value[Y - 2 : Y - 1, :]
         visc[i] = value
     launch_down("yv")
     launch_up("yv")
 
-    row_id = lax.broadcasted_iota(jnp.int32, (Y, Z), 0)
-    lane_id = lax.broadcasted_iota(jnp.int32, (Y, Z), 1)
-    first_row, last_row = row_id == 0, row_id == Y - 1
+    row_id = lax.broadcasted_iota(jnp.int32, (X, Z), 0)
+    lane_id = lax.broadcasted_iota(jnp.int32, (1, Z), 1)
+    first_row, last_row = row_id == 0, row_id == X - 1
     first_lane, last_lane = lane_id == 0, lane_id == Z - 1
 
-    def y_next(plane, halo):
-        return jnp.where(last_row, halo, pltpu.roll(plane, Y - 1, 0))
-
-    def y_prev(plane, halo):
+    def y_next(plane):
+        return pltpu.roll(plane, Y - 1, 0)
+
+    def y_prev(plane):
+        return pltpu.roll(plane, 1, 0)
+
+    def x_next(plane, halo):
+        return jnp.where(last_row, halo, pltpu.roll(plane, X - 1, 0))
+
+    def x_prev(plane, halo):
         return jnp.where(first_row, halo, pltpu.roll(plane, 1, 0))
 
     def z_next(plane):
@@ -299,61 +359,90 @@
     def z_prev(plane):
         return pltpu.roll(plane, 1, 1)
 
+    def z_coefs(v):
+        z_up = jnp.where(last_lane, 0.0, 0.5 * (v + z_next(v)))
+        edge = jnp.where(first_lane | last_lane, 0.5 * v, 0.0)
+        return z_up, z_prev(z_up), edge
+
+    def update(coefs, scale, source, value, nexts, prevs, v):
+        press = value[3]
+        divergence = source[3]
+        results = []
+        for c in range(3):
+            u = value[c]
+            above = [nexts(c, d) for d in range(3)]
+            below = [prevs(c, d) for d in range(3)]
+            total = coefs[0] * above[0] + coefs[1] * below[0]
+            total = total + coefs[2] * above[1] + coefs[3] * below[1]
+            total = total + coefs[4] * above[2] + coefs[5] * below[2]
+            ahead, behind = nexts(3, c), below[c]
+            if c == 2:
+                ahead = jnp.where(last_lane, 0.0, ahead)
+                behind = jnp.where(first_lane, 0.0, behind)
+            residual = source[c] + total - (ahead - press)
+            results.append((1.0 - RELAX_VELOCITY) * u + scale * residual)
+            divergence = divergence + (u - behind)
+        results.append(press - RELAX_PRESSURE * v * divergence)
+        return results
+
+    def sweep(field, x):
+        i = x + 1
+        value = [field[c, i] for c in range(4)]
+
+        def nexts(c, d):
+            return (lambda: field[c, i + 1], lambda: y_next(value[c]), lambda: z_next(value[c]))[d]()
+
+        def prevs(c, d):
+            return (lambda: field[c, i - 1], lambda: y_prev(value[c]), lambda: z_prev(value[c]))[d]()
+
+        coefs = (cx[i], cx[i - 1], cyu[x], cyl[x], czu[x], czl[x])
+        source = [src[c, x] for c in range(4)]
+        return update(coefs, rec[x], source, value, nexts, prevs, visc[i])
+
+    def face_sweep(side, field, inner, outer, low_row, high_row):
+        value = [field[side, c] for c in range(4)]
+
+        def nexts(c, d):
+            if d == 0:
+                return x_next(value[c], high_row(c))
+            if d == 1:
+                return (inner if side == 0 else outer)[side, c]
+            return z_next(value[c])
+
+        def prevs(c, d):
+            if d == 0:
+                return x_prev(value[c], low_row(c))
+            if d == 1:
+                return (outer if side == 0 else inner)[side, c]
+            return z_prev(value[c])
+
+        coefs = [fc[side, k] for k in range(6)]
+        source = [fsrc[side, c] for c in range(4)]
+        return update(coefs, fc[side, 6], source, value, nexts, prevs, ysv[side])
+
     for i in range(X + 1):
         cx[i] = 0.5 * (visc[i] + visc[i + 1])
-
-    own_src.wait()
-    arrive("yv")
-    for x in range(X):
+    arrive("x0")
+
+    def first(x):
         v = visc[x + 1]
-        half = 0.5 * v
-        y_up = 0.5 * (v + y_next(v, yrv[1, x : x + 1, :]))
-        y_down = 0.5 * (v + y_prev(v, yrv[0, x : x + 1, :]))
-        z_up = jnp.where(last_lane, 0.0, 0.5 * (v + z_next(v)))
-        z_down = z_prev(z_up)
-        edge = jnp.where(first_lane | last_lane, half, 0.0)
-        diagonal = cx[x] + cx[x + 1] + y_up + y_down + z_up + z_down + edge
+        y_up = 0.5 * (v + y_next(v))
+        y_down = 0.5 * (v + y_prev(v))
+        z_up, z_down, edge = z_coefs(v)
         cyu[x] = y_up
         cyl[x] = y_down
         czu[x] = z_up
         czl[x] = z_down
-        rec[x] = RELAX_VELOCITY / diagonal
-    arrive("y0")
-    arrive("x0")
-
-    def sweep(field, halo, x):
-        i = x + 1
-        press = field[3, i]
-        scale = rec[x]
-        divergence = src[3, x]
-        results = []
-        for c in range(3):
-            u = field[c, i]
-            below_x = field[c, i - 1]
-            below_y = y_prev(u, halo[0, c, x : x + 1, :])
-            below_z = z_prev(u)
-            total = cx[i] * field[c, i + 1] + cx[i - 1] * below_x
-            total = total + cyu[x] * y_next(u, halo[1, c, x : x + 1, :]) + cyl[x] * below_y
-            total = total + czu[x] * z_next(u) + czl[x] * below_z
-            if c == 0:
-                ahead, behind = field[3, i + 1], below_x
-            elif c == 1:
-                ahead, behind = y_next(press, halo[1, 3, x : x + 1, :]), below_y
-            else:
-                ahead = jnp.where(last_lane, 0.0, z_next(press))
-                behind = jnp.where(first_lane, 0.0, below_z)
-            residual = src[c, x] + total - (ahead - press)
-            results.append((1.0 - RELAX_VELOCITY) * u + scale * residual)
-            divergence = divergence + (u - behind)
-        results.append(press - RELAX_PRESSURE * visc[i] * divergence)
-        return results
-
-    def first(x):
-        for c, plane in enumerate(sweep(f0, yr, x)):
+        rec[x] = RELAX_VELOCITY / (cx[x] + cx[x + 1] + y_up + y_down + z_up + z_down + edge)
+        for c, plane in enumerate(sweep(f0, x)):
             f1[c, x + 1] = plane
-            ys2[0, c, x : x + 1, :] = plane[0:1, :]
-            if c < 3:
-                ys2[1, c, x : x + 1, :] = plane[Y - 1 : Y, :]
+            if x == 0:
+                xs[0, c] = plane
+            if x == X - 1:
+                xs[1, c] = plane
+            for side in range(2):
+                row = inners[side]
+                fin2[side, c, x : x + 1, :] = plane[row : row + 1, :]
 
     first(0)
     launch_down("x1")
@@ -361,12 +450,48 @@
     launch_up("x1")
     for x in range(1, X - 1):
         first(x)
-    launch_down("y1")
-    launch_up("y1")
-    arrive("y1")
+
+    arrive("y0")
+    arrive("yv")
+    for side in range(2):
+        y = edges[side]
+        v = ysv[side]
+        above, below = (vin, yrv) if side == 0 else (yrv, vin)
+        x_up = 0.5 * (v + x_next(v, visc[X + 1, y : y + 1, :]))
+        x_down = 0.5 * (v + x_prev(v, visc[0, y : y + 1, :]))
+        y_up = 0.5 * (v + above[side])
+        y_down = 0.5 * (v + below[side])
+        z_up, z_down, edge = z_coefs(v)
+        total = x_up + x_down + y_up + y_down + z_up + z_down + edge
+        for k, coef in enumerate((x_up, x_down, y_up, y_down, z_up, z_down)):
+            fc[side, k] = coef
+        fc[side, 6] = RELAX_VELOCITY / total
+        planes = face_sweep(
+            side,
+            ys,
+            fin,
+            yr,
+            lambda c: f0[c, 0, y : y + 1, :],
+            lambda c: f0[c, X + 1, y : y + 1, :],
+        )
+        for c, plane in enumerate(planes):
+            ys2[side, c] = plane
+            xrs[0, side * 4 + c : side * 4 + c + 1, :] = plane[0:1, :]
+            xrs[1, side * 4 + c : side * 4 + c + 1, :] = plane[X - 1 : X, :]
+        if side == 0:
+            launch_down("y1")
+        else:
+            launch_up("y1")
+            launch_down("xr")
+            launch_up("xr")
+    for side in range(2):
+        y = edges[side]
+        for c in range(4):
+            for x in range(X):
+                f1[c, x + 1, y : y + 1, :] = ys2[side, c, x : x + 1, :]
 
     def second(x):
-        planes = sweep(f1, yr2, x)
+        planes = sweep(f1, x)
         for c, plane in enumerate(planes):
             out_ref[c, x] = plane
         sens_ref[x] = dens[x] * planes[2]
@@ -377,10 +502,38 @@
     second(0)
     second(X - 1)
 
+    arrive("y1")
+    arrive("xr")
+    for side in range(2):
+        y = edges[side]
+        planes = face_sweep(
+            side,
+            ys2,
+            fin2,
+            yr2,
+            lambda c: xr[0, side * 4 + c : side * 4 + c + 1, :],
+            lambda c: xr[1, side * 4 + c : side * 4 + c + 1, :],
+        )
+        for x in range(X):
+            for c, plane in enumerate(planes):
+                out_ref[c, x, y : y + 1, :] = plane[x : x + 1, :]
+            sens_ref[x, y : y + 1, :] = dens[x, y : y + 1, :] * planes[2][x : x + 1, :]
+
     for copy in w_copies + m_copies:
         copy.wait_send()
     for name in pairs:
         sent(name)
+
+
+def flush(end, sens, end_h, sens_h, sem):
+    copies = [
+        pltpu.make_async_copy(end.at[c], end_h.at[c], sem.at[c]) for c in range(end.shape[0])
+    ]
+    copies.append(pltpu.make_async_copy(sens, sens_h, sem.at[end.shape[0]]))
+    for copy in copies:
+        copy.start()
+    for copy in copies:
+        copy.wait()
 
 
 def on_device(n, m, *arrays):
@@ -391,20 +544,23 @@
     W = -(-rows // 128) * 128
     f32 = jnp.float32
     vmem = pl.BlockSpec(memory_space=pltpu.VMEM)
-    smem = pl.BlockSpec(memory_space=pltpu.SMEM)
-    anywhere = pl.BlockSpec(memory_space=pl.ANY)
+    hbm = pl.BlockSpec(memory_space=pltpu.HBM)
     block = pltpu.VMEM((X, Y, Z), f32)
     padded = pltpu.VMEM((X + 2, Y, Z), f32)
     faces = pltpu.VMEM((2, 4, X, Z), f32)
     face = pltpu.VMEM((2, X, Z), f32)
     dma = pltpu.SemaphoreType.DMA
-    return pl.pallas_call(
+    pinned = [
+        array if array.ndim == 2 else pltpu.with_memory_space_constraint(array, pltpu.HBM)
+        for array in arrays
+    ]
+    end, sens = pl.pallas_call(
         functools.partial(kernel, n, m),
         out_shape=(
             jax.ShapeDtypeStruct((4, X, Y, Z), f32),
             jax.ShapeDtypeStruct((X, Y, Z), f32),
         ),
-        in_specs=[anywhere] * 5 + [vmem] * 3 + [smem] * 3,
+        in_specs=[hbm] * 8 + [pl.BlockSpec(memory_space=pltpu.SMEM)] + [hbm] * 2,
         out_specs=(vmem, vmem),
         scratch_shapes=[
             pltpu.VMEM((4, X + 2, Y, Z), f32),
@@ -430,18 +586,42 @@
             face,
             faces,
             faces,
-            dma((5,)),
+            faces,
+            faces,
+            faces,
+            face,
+            pltpu.VMEM((2, 7, X, Z), f32),
+            pltpu.VMEM((2, 4, Y, Z), f32),
+            pltpu.VMEM((2, 8, Z), f32),
+            pltpu.VMEM((2, 8, Z), f32),
+            pltpu.VMEM((1, 1, B), jnp.int32),
+            pltpu.VMEM((1, 1, B), jnp.int32),
+            pltpu.VMEM((1, 1, B), jnp.int32),
+            pltpu.SMEM(arrays[9].shape, f32),
+            pltpu.SMEM(arrays[10].shape, f32),
+            dma((10,)),
             dma((n,)),
             dma((n,)),
             dma((n,)),
             dma((n,)),
-            dma((12,)),
-            dma((12,)),
+            dma((14,)),
+            dma((14,)),
         ],
         compiler_params=pltpu.CompilerParams(
             collective_id=0, has_side_effects=True, vmem_limit_bytes=40 * 1024 * 1024
         ),
-    )(*arrays)
+    )(*pinned)
+    return pl.pallas_call(
+        flush,
+        out_shape=(
+            jax.ShapeDtypeStruct(end.shape, f32),
+            jax.ShapeDtypeStruct(sens.shape, f32),
+        ),
+        in_specs=[pl.BlockSpec(memory_space=pl.ANY)] * 2,
+        out_specs=(hbm, hbm),
+        compiler_params=pltpu.CompilerParams(vmem_limit_bytes=1024 * 1024),
+        scratch_shapes=[dma((5,))],
+    )(end, sens)
 
 
 def solution(mesh):

time: 25.7 us -> 18.4 us (0.72)
  local copies, waits for them, and re-layouts: 8.1 us -> 0 us
  Pallas kernels: 15.8 us -> 16.9 us
    unnamed x22 -> x0, local copies, waits for them, and re-layouts: 8.1 us -> none
    pallas_call x0 -> x1, Pallas kernels: none -> 1.09 us  [on_device(): pl.pallas_call(flush, out_shape=(jax.ShapeDtypeStruct(end.shape, f32), ja...]
where the time goes in v2:
time: 18.4 us; the launch traced here: 18.2 us
  Pallas kernels  16.9 us (92%)
  between operations  1.29 us (7%)
    pallas_call x1, Pallas kernels, on_device(): pl.pallas_call(functools.partial(kernel, n, m), out_shape=(jax.ShapeDtype...  15.8 us
    pallas_call x1, Pallas kernels, on_device(): pl.pallas_call(flush, out_shape=(jax.ShapeDtypeStruct(end.shape, f32), ja...  1.09 us

profile of v2, /device:TPU:1, one launch (start us, length us, event | category | flops | bytes accessed | tf_op | source)
XLA Modules:
  0.0 18.2 jit_solution(9450045526483216608)
XLA Ops:
  1.3 15.8 %shard_map.122 = (f32[4,16,16,256]{3,2,1,0:T(8,128)S(1)}, f32[16,16,256]{2,1,0:T(8,128)S(1)}) custom-call(f32[4,16,16,256]{3,2,1,0:T(8,128)} %start_h.1, f32[4,16,16,256]{3,2,1,0:T(8,128)} %source_h.1, f32[16,16,256]{2,1,0:T(8,128)} %bglog_h.1, f32[16,16,256]{2,1,0:T(8,128)} %bgden_h.1, f32[1,1,32,256]{3,2,1,0:T(8,128)} %weights_h.1, s32[1,1,32]{2,1,0:T(1,128)} %phase_h.1, ...), custom_call_target="tpu_custom_call" | custom-call | tf_op jit(solution)/shard_map/pallas_call | solution.py:557
  17.1 1.1 %shard_map.123 = (f32[4,16,16,256]{3,2,1,0:T(8,128)}, f32[16,16,256]{2,1,0:T(8,128)}) custom-call(f32[4,16,16,256]{3,2,1,0:T(8,128)S(1)} %get-tuple-element.4.end, f32[16,16,256]{2,1,0:T(8,128)S(1)} %get-tuple-element.5.sens), custom_call_target="tpu_custom_call" | custom-call | tf_op jit(solution)/shard_map/pallas_call | solution.py:614

commit v3 on v2

--- a/solution.py
+++ b/solution.py
@@ -268,8 +268,6 @@
 
     launch_down("bg")
     launch_up("bg")
-    launch_down("x0")
-    launch_up("x0")
 
     own_start.wait()
     for c in range(4):
@@ -292,6 +290,9 @@
         for c in range(4):
             for x in range(X):
                 fsrc[side, c, x : x + 1, :] = src[c, x, edges[side] : edges[side] + 1, :]
+
+    launch_down("x0")
+    launch_up("x0")
 
     own_w.wait()
     own_bg.wait()

time: 18.4 us -> 18.4 us (level)
  no operation moved by 1% of the time
where the time goes in v3:
time: 18.4 us; the launch traced here: 18.2 us
  Pallas kernels  16.9 us (92%)
  between operations  1.29 us (7%)
    pallas_call x1, Pallas kernels, on_device(): pl.pallas_call(functools.partial(kernel, n, m), out_shape=(jax.ShapeDtype...  15.8 us
    pallas_call x1, Pallas kernels, on_device(): pl.pallas_call(flush, out_shape=(jax.ShapeDtypeStruct(end.shape, f32), ja...  1.09 us

profile of v3, /device:TPU:1, one launch (start us, length us, event | category | flops | bytes accessed | tf_op | source)
XLA Modules:
  0.0 18.2 jit_solution(13980688839073537294)
XLA Ops:
  1.3 15.8 %shard_map.122 = (f32[4,16,16,256]{3,2,1,0:T(8,128)S(1)}, f32[16,16,256]{2,1,0:T(8,128)S(1)}) custom-call(f32[4,16,16,256]{3,2,1,0:T(8,128)} %start_h.1, f32[4,16,16,256]{3,2,1,0:T(8,128)} %source_h.1, f32[16,16,256]{2,1,0:T(8,128)} %bglog_h.1, f32[16,16,256]{2,1,0:T(8,128)} %bgden_h.1, f32[1,1,32,256]{3,2,1,0:T(8,128)} %weights_h.1, s32[1,1,32]{2,1,0:T(1,128)} %phase_h.1, ...), custom_call_target="tpu_custom_call" | custom-call | tf_op jit(solution)/shard_map/pallas_call | solution.py:558
  17.1 1.1 %shard_map.123 = (f32[4,16,16,256]{3,2,1,0:T(8,128)}, f32[16,16,256]{2,1,0:T(8,128)}) custom-call(f32[4,16,16,256]{3,2,1,0:T(8,128)S(1)} %get-tuple-element.4.end, f32[16,16,256]{2,1,0:T(8,128)S(1)} %get-tuple-element.5.sens), custom_call_target="tpu_custom_call" | custom-call | tf_op jit(solution)/shard_map/pallas_call | solution.py:615
